TPU v7x, 32 devices: a whole 2x2x4 slice. The times are simulated.
32 devices in a mesh: dp: 8 (over z, x), tensor: 4 (over y, core).
Axes of the slice: x: 2, y: 2, z: 4, core: 2. Of those that a mesh axis runs over, the one named last changes fastest.
Arguments:
- images: bfloat16 [16, 197, 768], P('dp'), may hold values from -6 to 6
- image_counts: int32 [8], P('dp'), may hold values from 1 to 2, as said below
- first_norm_gain: float32 [768], replicated, may hold values from 0.5 to 1.5
- first_norm_bias: float32 [768], replicated, may hold values from -3 to 3
- qkv_weight: bfloat16 [768, 3, 768], P(None, None, 'tensor'), may hold values from -2 to 2
- qv_bias: float32 [2, 768], P(None, 'tensor'), may hold values from -3 to 3
- out_weight: bfloat16 [768, 768], P('tensor'), may hold values from -1.25 to 1.25
- out_bias: float32 [768], replicated, may hold values from -3 to 3
- second_norm_gain: float32 [768], replicated, may hold values from 0.5 to 1.5
- second_norm_bias: float32 [768], replicated, may hold values from -3 to 3
- fc1_weight: bfloat16 [768, 3072], P(None, 'tensor'), may hold values from -0.21875 to 0.21875
- fc1_bias: float32 [3072], P('tensor'), may hold values from -3 to 3
- fc2_weight: bfloat16 [3072, 768], P('tensor'), may hold values from -0.15625 to 0.15625
- fc2_bias: float32 [768], replicated, may hold values from -3 to 3
- cotangent: bfloat16 [16, 197, 768], P('dp'), may hold values from -6 to 6
Outputs:
- block_out: bfloat16 [16, 197, 768], P('dp')
- input_grad: bfloat16 [16, 197, 768], P('dp')
- grad_first_norm_gain: float32 [768], replicated
- grad_first_norm_bias: float32 [768], replicated
- grad_qkv_weight: float32 [768, 3, 768], P(None, None, 'tensor')
- grad_qv_bias: float32 [2, 768], P(None, 'tensor')
- grad_out_weight: float32 [768, 768], P('tensor')
- grad_out_bias: float32 [768], replicated
- grad_second_norm_gain: float32 [768], replicated
- grad_second_norm_bias: float32 [768], replicated
- grad_fc1_weight: float32 [768, 3072], P(None, 'tensor')
- grad_fc1_bias: float32 [3072], P('tensor')
- grad_fc2_weight: float32 [3072, 768], P('tensor')
- grad_fc2_bias: float32 [768], replicated
Inputs may be any that keep to these rules, and one draw needn't show every extreme that they name: `image_counts`: some index of dp has 2 live slots and some has 1; live slots come first in each index's block of 2.
All inputs are finite; a program needn't handle non-finite values.
Results may differ from a plain program's by a relative error of at most 0.02.
Values may be sent and summed in bfloat16 or wider, within the bound.
A program may use at most 128 MiB of HBM per device.

v0:
```python
import jax
import jax.numpy as jnp
from jax import lax
from jax.sharding import PartitionSpec as P

HEAD_DIM = 64
EPS = 1e-06
ROOT_HALF = 0.7071067811865476
INV_ROOT_TAU = 0.3989422804014327


def to_half(array_in):
    return array_in.astype(jnp.bfloat16)


def norm_forward(row_values, gain_vec, shift_vec):
    centre = row_values - jnp.mean(row_values, axis=-1, keepdims=True)
    inverse = lax.rsqrt(jnp.mean(centre * centre, axis=-1, keepdims=True) + EPS)
    scaled = centre * inverse
    return (scaled * gain_vec + shift_vec, scaled, inverse)


def norm_backward(grad_out, scaled, inverse, gain_vec):
    grad_scaled = grad_out * gain_vec
    grad_rows = inverse * (
        grad_scaled
        - jnp.mean(grad_scaled, axis=-1, keepdims=True)
        - scaled * jnp.mean(grad_scaled * scaled, axis=-1, keepdims=True)
    )
    return (grad_rows, jnp.sum(grad_out * scaled, axis=0), jnp.sum(grad_out, axis=0))


def gelu_value(pre_act):
    return 0.5 * pre_act * (1.0 + jax.scipy.special.erf(pre_act * ROOT_HALF))


def gelu_slope(pre_act):
    return (
        0.5 * (1.0 + jax.scipy.special.erf(pre_act * ROOT_HALF))
        + pre_act * jnp.exp(-0.5 * pre_act * pre_act) * INV_ROOT_TAU
    )


def per_device(
    images,
    image_counts,
    first_norm_gain,
    first_norm_bias,
    qkv_weight,
    qv_bias,
    out_weight,
    out_bias,
    second_norm_gain,
    second_norm_bias,
    fc1_weight,
    fc1_bias,
    fc2_weight,
    fc2_bias,
    cotangent,
):
    f32 = jnp.float32
    slot_count, length, model_width = images.shape
    local_width = qkv_weight.shape[2]
    local_heads = local_width // HEAD_DIM
    row_count = slot_count * length
    score_scale = HEAD_DIM ** (-0.5)
    live_slots = (jnp.arange(slot_count, dtype=jnp.int32) < image_counts[0]).astype(f32)
    row_live = jnp.broadcast_to(live_slots[:, None], (slot_count, length)).reshape(row_count, 1)
    head_shape = (slot_count, length, local_heads, HEAD_DIM)
    row_values = images.reshape(row_count, model_width).astype(f32)
    norm_one, scaled_one, inverse_one = norm_forward(row_values, first_norm_gain, first_norm_bias)
    norm_one = to_half(norm_one)
    qkv_flat = qkv_weight.reshape(model_width, 3 * local_width)
    qkv_shift = jnp.stack([qv_bias[0], jnp.zeros_like(qv_bias[0]), qv_bias[1]])
    qkv_rows = to_half(
        jnp.dot(norm_one, qkv_flat, preferred_element_type=f32).reshape(row_count, 3, local_width)
        + qkv_shift
    )
    queries = qkv_rows[:, 0].reshape(head_shape)
    key_heads = qkv_rows[:, 1].reshape(head_shape)
    value_heads = qkv_rows[:, 2].reshape(head_shape)
    scores = (
        jnp.einsum("bqhd,bkhd->bhqk", queries, key_heads, preferred_element_type=f32) * score_scale
    )
    row_peak = jnp.max(scores, axis=-1, keepdims=True)
    log_total = row_peak + jnp.log(jnp.sum(jnp.exp(scores - row_peak), axis=-1, keepdims=True))
    probs_full = jnp.exp(scores - log_total)
    probs_half = to_half(probs_full)
    context = to_half(
        jnp.einsum("bhqk,bkhd->bqhd", probs_half, value_heads, preferred_element_type=f32)
    )
    context_rows = context.reshape(row_count, local_width)
    attn_part = jnp.dot(context_rows, out_weight, preferred_element_type=f32)
    resid_rows = (
        row_values
        + lax.psum(attn_part.astype(jnp.bfloat16), "tensor").astype(jnp.float32)
        + out_bias
    )
    norm_two, scaled_two, inverse_two = norm_forward(resid_rows, second_norm_gain, second_norm_bias)
    norm_two = to_half(norm_two)
    pre_act = jnp.dot(norm_two, fc1_weight, preferred_element_type=f32) + fc1_bias
    act_half = to_half(gelu_value(pre_act))
    mlp_part = jnp.dot(act_half, fc2_weight, preferred_element_type=f32)
    final_rows = (
        resid_rows
        + lax.psum(mlp_part.astype(jnp.bfloat16), "tensor").astype(jnp.float32)
        + fc2_bias
    )
    block_out = to_half(final_rows * row_live).reshape(slot_count, length, model_width)
    inv_images = 1.0 / (slot_count * lax.axis_size("dp"))
    grad_final = cotangent.reshape(row_count, model_width).astype(f32) * row_live
    grad_final_half = to_half(grad_final)
    grad_act = jnp.dot(grad_final_half, fc2_weight.T, preferred_element_type=f32)
    grad_pre = grad_act * gelu_slope(pre_act)
    grad_pre_half = to_half(grad_pre)
    two_part = jnp.dot(grad_pre_half, fc1_weight.T, preferred_element_type=f32)
    grad_norm_two = lax.psum(two_part.astype(jnp.bfloat16), "tensor").astype(jnp.float32)
    back_two, gain_two, shift_two = norm_backward(
        grad_norm_two, scaled_two, inverse_two, second_norm_gain
    )
    mlp_grads = (
        jnp.dot(norm_two.T, grad_pre_half, preferred_element_type=f32) * inv_images,
        jnp.sum(grad_pre, axis=0, keepdims=True) * inv_images,
        jnp.dot(act_half.T, grad_final_half, preferred_element_type=f32) * inv_images,
        jnp.stack([gain_two, shift_two, jnp.sum(grad_final, axis=0)]) * inv_images,
    )
    grad_resid = grad_final + back_two
    grad_resid_half = to_half(grad_resid)
    grad_context = to_half(
        jnp.dot(grad_resid_half, out_weight.T, preferred_element_type=f32)
    ).reshape(head_shape)
    grad_probs = jnp.einsum(
        "bqhd,bkhd->bhqk", grad_context, value_heads, preferred_element_type=f32
    )
    grad_scores = to_half(
        probs_full
        * (grad_probs - jnp.sum(probs_full * grad_probs, axis=-1, keepdims=True))
        * score_scale
    )
    grad_queries = jnp.einsum(
        "bhqk,bkhd->bqhd", grad_scores, key_heads, preferred_element_type=f32
    ).reshape(row_count, local_width)
    grad_keys = jnp.einsum(
        "bhqk,bqhd->bkhd", grad_scores, queries, preferred_element_type=f32
    ).reshape(row_count, local_width)
    grad_values = jnp.einsum(
        "bhqk,bqhd->bkhd", probs_half, grad_context, preferred_element_type=f32
    ).reshape(row_count, local_width)
    grad_qkv_half = to_half(jnp.stack([grad_queries, grad_keys, grad_values], axis=1)).reshape(
        row_count, 3 * local_width
    )
    one_part = jnp.dot(grad_qkv_half, qkv_flat.T, preferred_element_type=f32)
    grad_norm_one = lax.psum(one_part.astype(jnp.bfloat16), "tensor").astype(jnp.float32)
    back_one, gain_one, shift_one = norm_backward(
        grad_norm_one, scaled_one, inverse_one, first_norm_gain
    )
    input_grad = to_half(grad_resid + back_one).reshape(slot_count, length, model_width)
    attn_grads = (
        jnp.dot(norm_one.T, grad_qkv_half, preferred_element_type=f32) * inv_images,
        jnp.stack([jnp.sum(grad_queries, axis=0), jnp.sum(grad_values, axis=0)]) * inv_images,
        jnp.dot(context_rows.T, grad_resid_half, preferred_element_type=f32) * inv_images,
        jnp.stack([gain_one, shift_one, jnp.sum(grad_resid, axis=0)]) * inv_images,
    )
    shares = (
        lax.psum_scatter(attn_grads[0], "dp", scatter_dimension=1, tiled=True),
        lax.psum_scatter(attn_grads[1], "dp", scatter_dimension=1, tiled=True),
        lax.psum_scatter(attn_grads[2], "dp", scatter_dimension=1, tiled=True),
        lax.psum_scatter(attn_grads[3], "dp", scatter_dimension=1, tiled=True),
        lax.psum_scatter(mlp_grads[0], "dp", scatter_dimension=1, tiled=True),
        lax.psum_scatter(mlp_grads[1], "dp", scatter_dimension=1, tiled=True),
        lax.psum_scatter(mlp_grads[2], "dp", scatter_dimension=1, tiled=True),
        lax.psum_scatter(mlp_grads[3], "dp", scatter_dimension=1, tiled=True),
    )
    gathered = (
        lax.all_gather(shares[0].astype(jnp.bfloat16), "dp", axis=1, tiled=True).astype(
            jnp.float32
        ),
        lax.all_gather(shares[1].astype(jnp.bfloat16), "dp", axis=1, tiled=True).astype(
            jnp.float32
        ),
        lax.all_gather(shares[2].astype(jnp.bfloat16), "dp", axis=1, tiled=True).astype(
            jnp.float32
        ),
        lax.all_gather(shares[3].astype(jnp.bfloat16), "dp", axis=1, tiled=True).astype(
            jnp.float32
        ),
        lax.all_gather(shares[4].astype(jnp.bfloat16), "dp", axis=1, tiled=True).astype(
            jnp.float32
        ),
        lax.all_gather(shares[5].astype(jnp.bfloat16), "dp", axis=1, tiled=True).astype(
            jnp.float32
        ),
        lax.all_gather(shares[6].astype(jnp.bfloat16), "dp", axis=1, tiled=True).astype(
            jnp.float32
        ),
        lax.all_gather(shares[7].astype(jnp.bfloat16), "dp", axis=1, tiled=True).astype(
            jnp.float32
        ),
    )
    attn_full = gathered[:4]
    mlp_full = gathered[4:]
    return (
        block_out,
        input_grad,
        attn_full[3][0],
        attn_full[3][1],
        attn_full[0].reshape(model_width, 3, local_width),
        attn_full[1],
        attn_full[2],
        attn_full[3][2],
        mlp_full[3][0],
        mlp_full[3][1],
        mlp_full[0],
        mlp_full[1][0],
        mlp_full[2],
        mlp_full[3][2],
    )


def solution(mesh):
    placed = (
        P("dp", None, None),
        P("dp"),
        P(),
        P(),
        P(None, None, "tensor"),
        P(None, "tensor"),
        P("tensor", None),
        P(),
        P(),
        P(),
        P(None, "tensor"),
        P("tensor"),
        P("tensor", None),
        P(),
        P("dp", None, None),
    )
    return jax.shard_map(
        per_device,
        mesh=mesh,
        in_specs=placed,
        out_specs=(
            P("dp", None, None),
            P("dp", None, None),
            P(),
            P(),
            P(None, None, "tensor"),
            P(None, "tensor"),
            P("tensor", None),
            P(),
            P(),
            P(),
            P(None, "tensor"),
            P("tensor"),
            P("tensor", None),
            P(),
        ),
        check_vma=False,
    )
```

profile of v0, /device:TPU:0, one launch (start us, length us, event | category | flops | bytes accessed | tf_op | source)
XLA Modules:
  0.0 741.2 jit_solution(13153335465204012786)
XLA Ops:
  25.3 33.3 %all-reduce.7.cloned.1.call-done = bf16[394,768]{1,0:T(8,128)(2,1)} async-done(((bf16[394,768]{1,0:T(8,128)(2,1)}), bf16[394,768]{1,0:T(8,128)(2,1)}) %all-reduce.7.cloned.1.call-update) | async-done | bytes 605200 | tf_op jit(solution)/shard_map/psum | solution.py:96
  69.7 31.1 %all-reduce.9.cloned.1.call-done = bf16[394,768]{1,0:T(8,128)(2,1)} async-done(((bf16[394,768]{1,0:T(8,128)(2,1)}), bf16[394,768]{1,0:T(8,128)(2,1)}) %all-reduce.9.cloned.1.call-update) | async-done | bytes 605200 | tf_op jit(solution)/shard_map/psum | solution.py:117
  107.8 4.5 fusion.69
  112.3 3.8 fusion.34
  130.3 3.4 convolution_multiply_fusion.1
  137.3 3.6 convolution_multiply_fusion
  142.0 26.2 %all-reduce.11.cloned.1.call-done = (bf16[394,768]{1,0:T(8,128)(2,1)}, bf16[394,768]{1,0:T(8,128)(2,1)}) async-done(((bf16[394,768]{1,0:T(8,128)(2,1)}, bf16[394,768]{1,0:T(8,128)(2,1)}), (bf16[394,768]{1,0:T(8,128)(2,1)}, bf16[394,768]{1,0:T(8,128)(2,1)})) %all-reduce.11.cloned.1.call-update) | async-done | bytes 1210384 | tf_op jit(solution)/shard_map/psum | solution.py:106
  177.2 3.1 convolution_multiply_fusion.2
  180.4 61.4 %reduce-scatter.19.cloned.1.call-done = f32[768,96]{0,1:T(8,128)} async-done(((f32[768,768]{0,1:T(8,128)}), f32[768,96]{0,1:T(8,128)}) %reduce-scatter.19.cloned.1.call-update) | async-done | bytes 294928 | tf_op jit(solution)/shard_map/reduce_scatter | solution.py:169
  245.3 60.9 %reduce-scatter.29.cloned.1.call-done = f32[96,1]{1,0:T(8,128)} async-done(((f32[768,1]{1,0:T(8,128)}), f32[96,1]{1,0:T(8,128)}) %reduce-scatter.29.cloned.1.call-update) | async-done | bytes 400
  307.3 19.5 %all-reduce = bf16[768]{0:T(1024)(128)(2,1)S(1)} all-reduce(bf16[768]{0:T(1024)(128)(2,1)S(1)} %dynamic-update-slice), channel_id=1, replica_groups=mesh['dp'=8,'tensor'=4] {'dp'}, use_global_device_ids=true, to_apply=%add | all-reduce | flops 768 | bytes 3072
  327.6 17.2 %all-reduce.1 = bf16[2,192]{1,0:T(2,128)(2,1)S(1)} all-reduce(f32[2,192]{1,0:T(2,128)S(1)} %maximum_multiply_fusion.2), channel_id=4, replica_groups=mesh['dp'=8,'tensor'=4] {'dp'}, use_global_device_ids=true, to_apply=%region_22.0.clone | all-reduce | flops 384 | bytes 2304
  344.8 18.3 %all-gather.1 = bf16[8,24,2]{1,2,0:T(2,128)(2,1)S(1)} all-gather(bf16[1,24,2]{1,2,0:T(2,128)(2,1)S(1)} %fusion.60), channel_id=1, replica_groups=mesh['dp'=8,'tensor'=4] {'dp'}, dimensions={0}, use_global_device_ids=true | all-gather | bytes 864 | tf_op jit(solution)/shard_map/all_gather | solution.py:178
  363.8 7.4 %reduce-scatter.27.cloned.1.call-done = f32[96,3]{1,0:T(8,128)} async-done(((f32[768,3]{1,0:T(8,128)}), f32[96,3]{1,0:T(8,128)}) %reduce-scatter.27.cloned.1.call-update) | async-done | bytes 1168
  372.1 19.0 %all-gather.2 = bf16[8,96,3]{1,2,0:T(4,128)(2,1)S(1)} all-gather(bf16[1,96,3]{1,2,0:T(4,128)(2,1)S(1)} %bitcast.107), channel_id=1, replica_groups=mesh['dp'=8,'tensor'=4] {'dp'}, dimensions={0}, use_global_device_ids=true | all-gather | bytes 5184 | tf_op jit(solution)/shard_map/all_gather | solution.py:196
  391.1 52.8 %reduce-scatter.21.cloned.1.call-done = f32[768,96]{0,1:T(8,128)} async-done(((f32[768,768]{0,1:T(8,128)}), f32[768,96]{0,1:T(8,128)}) %reduce-scatter.21.cloned.1.call-update) | async-done | bytes 294928 | tf_op jit(solution)/shard_map/reduce_scatter | solution.py:171
  456.9 51.7 %reduce-scatter.23.cloned.1.call-done = f32[96,3]{1,0:T(8,128)} async-done(((f32[768,3]{1,0:T(8,128)}), f32[96,3]{1,0:T(8,128)}) %reduce-scatter.23.cloned.1.call-update) | async-done | bytes 1168
  509.4 18.7 %all-gather = bf16[8,96,3]{1,2,0:T(4,128)(2,1)S(1)} all-gather(bf16[1,96,3]{1,2,0:T(4,128)(2,1)S(1)} %bitcast.108), channel_id=1, replica_groups=mesh['dp'=8,'tensor'=4] {'dp'}, dimensions={0}, use_global_device_ids=true | all-gather | bytes 5184 | tf_op jit(solution)/shard_map/all_gather | solution.py:184
  528.8 45.3 %reduce-scatter.25.cloned.1.call-done = f32[96,192]{1,0:T(8,128)} async-done(((f32[768,192]{1,0:T(8,128)}), f32[96,192]{1,0:T(8,128)}) %reduce-scatter.25.cloned.1.call-update) | async-done | bytes 73744
  575.2 31.8 %all_gather.27 = bf16[192,768]{0,1:T(8,128)(2,1)S(1)} all-gather(bf16[192,96]{0,1:T(8,128)(2,1)S(1)} %copy.157), channel_id=1, replica_groups=mesh['dp'=8,'tensor'=4] {'dp'}, dimensions={1}, use_global_device_ids=true | all-gather | bytes 331776 | tf_op jit(solution)/shard_map/all_gather | solution.py:181
  608.0 36.5 %reduce-scatter.17.cloned.1.call-done = f32[768,72]{0,1:T(8,128)} async-done(((f32[768,576]{0,1:T(8,128)}), f32[768,72]{0,1:T(8,128)}) %reduce-scatter.17.cloned.1.call-update) | async-done | bytes 221200 | tf_op jit(solution)/shard_map/reduce_scatter | solution.py:165
  645.4 33.5 %all_gather.25 = bf16[768,576]{0,1:T(8,128)(2,1)S(1)} all-gather(bf16[768,72]{0,1:T(8,128)(2,1)S(1)} %convert_element_type.185), channel_id=1, replica_groups=mesh['dp'=8,'tensor'=4] {'dp'}, dimensions={1}, use_global_device_ids=true | all-gather | bytes 995328 | tf_op jit(solution)/shard_map/all_gather | solution.py:175
  680.3 8.9 %all-gather.6.cloned.1.call-done = bf16[768,768]{0,1:T(8,128)(2,1)} async-done(((bf16[768,96]{0,1:T(8,128)(2,1)}), bf16[768,768]{0,1:T(8,128)(2,1)}) %all-gather.6.cloned.1.call-update) | async-done | bytes 1179664 | tf_op jit(solution)/shard_map/all_gather | solution.py:187
  691.9 39.8 %all-gather.8.cloned.1.call-done = bf16[768,768]{0,1:T(8,128)(2,1)} async-done(((bf16[768,96]{0,1:T(8,128)(2,1)}), bf16[768,768]{0,1:T(8,128)(2,1)}) %all-gather.8.cloned.1.call-update) | async-done | bytes 1179664 | tf_op jit(solution)/shard_map/all_gather | solution.py:193
  (212 shorter events, 92.9 us)
Async XLA Ops:
  7.2 53.4 %copy-start = (bf16[768,768]{1,0:T(8,128)(2,1)S(1)}, bf16[768,768]{1,0:T(8,128)(2,1)}, u32[]{:S(2)}) copy-start(bf16[768,768]{1,0:T(8,128)(2,1)} %param.25) | copy-start | bytes 3538948
  7.2 3.0 copy-start.24
  7.2 3.0 copy-start.22
  7.2 51.3 %all-reduce.7.cloned.1.call-start = ((), (), s32[]{:S(2)}) async-start(), calls=%async_computation.7 | async-start | bytes 1228800 | tf_op jit(solution)/shard_map/psum | solution.py:96
  21.9 78.9 %all-reduce.9.cloned.1.call-start = ((), (), s32[]{:S(2)}) async-start(), calls=%async_computation.8 | async-start | bytes 1228800 | tf_op jit(solution)/shard_map/psum | solution.py:117
  23.3 35.3 %copy-start.25 = (f32[768]{0:T(1024)S(1)}, f32[768]{0:T(1024)}, u32[]{:S(2)}) copy-start(f32[768]{0:T(1024)} %param.22) | copy-start | bytes 9220
  25.1 35.1 %copy-start.31 = (f32[2]{0:T(128)}, f32[2]{0:T(128)S(1)}, u32[]{:S(2)}) copy-start(f32[2]{0:T(128)S(1)} %compare_convert_fusion) | copy-start | bytes 28
  66.5 101.7 %all-reduce.11.cloned.1.call-start = ((), (), s32[]{:S(2)}) async-start(), calls=%async_computation.18 | async-start | bytes 2457600 | tf_op jit(solution)/shard_map/psum | solution.py:106
  107.8 4.5 copy-start.19
  129.6 112.1 %reduce-scatter.19.cloned.1.call-start = ((), (), s32[]{:S(2)}) async-start(), calls=%async_computation.10 | async-start | bytes 2654208 | tf_op jit(solution)/shard_map/reduce_scatter | solution.py:169
  133.7 172.5 %reduce-scatter.29.cloned.1.call-start = ((), (), s32[]{:S(2)}) async-start(), calls=%async_computation.17 | async-start | bytes 442368
  136.2 235.0 %reduce-scatter.27.cloned.1.call-start = ((), (), s32[]{:S(2)}) async-start(), calls=%async_computation.16 | async-start | bytes 442368
  137.2 306.7 %reduce-scatter.21.cloned.1.call-start = ((), (), s32[]{:S(2)}) async-start(), calls=%async_computation.12 | async-start | bytes 2654208 | tf_op jit(solution)/shard_map/reduce_scatter | solution.py:171
  140.9 367.6 %reduce-scatter.23.cloned.1.call-start = ((), (), s32[]{:S(2)}) async-start(), calls=%async_computation.14 | async-start | bytes 442368
  168.2 3.2 copy-start.14
  171.4 402.7 %reduce-scatter.25.cloned.1.call-start = ((), (), s32[]{:S(2)}) async-start(), calls=%async_computation.15 | async-start | bytes 884736
  176.2 468.3 %reduce-scatter.17.cloned.1.call-start = ((), (), s32[]{:S(2)}) async-start(), calls=%async_computation.9 | async-start | bytes 1990656 | tf_op jit(solution)/shard_map/reduce_scatter | solution.py:165
  180.3 63.2 %copy-start.28 = (u32[32]{0:T(128)S(1)}, u32[32]{0:T(128)}, u32[]{:S(2)}) copy-start(u32[32]{0:T(128)} %constant.41) | copy-start | bytes 388
  180.3 147.2 %copy-start.29 = (f32[3,64]{1,0:T(4,128)S(1)}, f32[3,64]{1,0:T(4,128)}, u32[]{:S(2)}) copy-start(f32[3,64]{1,0:T(4,128)} %get-tuple-element.107) | copy-start | bytes 2308
  180.3 266.0 %copy-start.26 = (f32[768]{0:T(1024)S(1)}, f32[768]{0:T(1024)}, u32[]{:S(2)}) copy-start(f32[768]{0:T(1024)} %param.28) | copy-start | bytes 9220
  180.3 508.8 %all-gather.6.cloned.1.call-start = ((), (), s32[]{:S(2)}) async-start(), calls=%async_computation.11 | async-start | bytes 1327104 | tf_op jit(solution)/shard_map/all_gather | solution.py:187
  243.4 488.2 %all-gather.8.cloned.1.call-start = ((), (), s32[]{:S(2)}) async-start(), calls=%async_computation.13 | async-start | bytes 1327104 | tf_op jit(solution)/shard_map/all_gather | solution.py:193
  446.3 6.7 copy-start.10
  448.5 4.6 copy-start.2
  (26 other events, 38.3 us)
Sparse Core Ops, SparseCore 0:
  22.0 36.4 all-reduce.6
  66.6 34.0 all-reduce.8
  129.7 38.4 all-reduce.10
  172.1 69.5 reduce-scatter.18
  244.8 61.3 reduce-scatter.28
  309.9 61.2 reduce-scatter.26
  375.3 68.6 reduce-scatter.20
  447.2 61.3 reduce-scatter.22
  511.9 62.2 reduce-scatter.24
  578.0 66.4 reduce-scatter.16
  646.7 42.4 all-gather.5
  691.2 40.3 all-gather.7
where the time goes:
time: 743 us; the launch traced here: 741 us
  waiting for transfers between devices  455 us (61%)
  blocking collectives  158 us (21%)
  local copies, waits for them, and re-layouts  47.1 us (6%)
  matrix products  41.1 us (6%)
  other arithmetic  22.2 us (3%)
  between operations  16.8 us (2%)
    unnamed x16, waiting for transfers between devices  166 us
    reduce_scatter x1, waiting for transfers between devices, per_device(): lax.psum_scatter(mlp_grads[0], 'dp', scatter_dimension=1, tiled=True)  61.4 us
    reduce_scatter x1, waiting for transfers between devices, per_device(): lax.psum_scatter(mlp_grads[2], 'dp', scatter_dimension=1, tiled=True)  52.8 us
    all_gather x1, waiting for transfers between devices, per_device(): lax.all_gather(shares[6].astype(jnp.bfloat16), 'dp', axis=1, tiled=True)  39.8 us
    unnamed x2, blocking collectives  36.6 us
    reduce_scatter x1, waiting for transfers between devices, per_device(): lax.psum_scatter(attn_grads[0], 'dp', scatter_dimension=1, tiled=True)  36.5 us
    all_gather x1, blocking collectives, per_device(): lax.all_gather(shares[0].astype(jnp.bfloat16), 'dp', axis=1, tiled=True)  33.5 us
    psum x1, waiting for transfers between devices, per_device(): lax.psum(attn_part.astype(jnp.bfloat16), 'tensor').astype(jnp.float32)  33.3 us
  transfers between devices with their start and end apart: 12, of which 12 were waited for; matrix products, arithmetic and copies ran while one was open for 7% of the time, Pallas kernels for 0%

commit v1 on v0

--- a/solution.py
+++ b/solution.py
@@ -190,9 +190,12 @@
         lax.all_gather(shares[5].astype(jnp.bfloat16), "dp", axis=1, tiled=True).astype(
             jnp.float32
         ),
-        lax.all_gather(shares[6].astype(jnp.bfloat16), "dp", axis=1, tiled=True).astype(
-            jnp.float32
-        ),
+        jnp.concatenate(
+            lax.all_to_all(
+                jnp.stack([shares[6].astype(jnp.bfloat16)] * lax.psum(1, "dp"), axis=0), "dp", 0, 0
+            ),
+            axis=1,
+        ).astype(jnp.float32),
         lax.all_gather(shares[7].astype(jnp.bfloat16), "dp", axis=1, tiled=True).astype(
             jnp.float32
         ),

time: 743 us -> 716 us (0.964)
  waiting for transfers between devices: 455 us -> 421 us
    all_gather x1 -> x0, waiting for transfers between devices: 39.8 us -> none  [per_device(): lax.all_gather(shares[6].astype(jnp.bfloat16), 'dp', axis=1, tiled=True)]
    reduce_scatter x1, waiting for transfers between devices: 61.4 us -> 82 us  [per_device(): lax.psum_scatter(mlp_grads[0], 'dp', scatter_dimension=1, tiled=True)]
    unnamed x16 -> x15, waiting for transfers between devices: 166 us -> 155 us
    unnamed x97 -> x99, local copies, waits for them, and re-layouts: 26.6 us -> 28 us
  transfers between devices with their start and end apart: 12 -> 12, of which waited for: 12 -> 11; matrix products, arithmetic and copies ran while one was open for 7% -> 8% of each run, Pallas kernels for 0% -> 0%
where the time goes in v1:
time: 716 us; the launch traced here: 714 us
  waiting for transfers between devices  421 us (59%)
  blocking collectives  158 us (22%)
  local copies, waits for them, and re-layouts  49.5 us (7%)
  matrix products  40.1 us (6%)
  other arithmetic  24.5 us (3%)
  between operations  16.4 us (2%)
    unnamed x15, waiting for transfers between devices  155 us
    reduce_scatter x1, waiting for transfers between devices, per_device(): lax.psum_scatter(mlp_grads[0], 'dp', scatter_dimension=1, tiled=True)  82 us
    reduce_scatter x1, waiting for transfers between devices, per_device(): lax.psum_scatter(mlp_grads[2], 'dp', scatter_dimension=1, tiled=True)  52.9 us
    unnamed x2, blocking collectives  36.7 us
    reduce_scatter x1, waiting for transfers between devices, per_device(): lax.psum_scatter(attn_grads[0], 'dp', scatter_dimension=1, tiled=True)  36.1 us
    all_gather x1, blocking collectives, per_device(): lax.all_gather(shares[0].astype(jnp.bfloat16), 'dp', axis=1, tiled=True)  33.5 us
    psum x1, waiting for transfers between devices, per_device(): lax.psum(attn_part.astype(jnp.bfloat16), 'tensor').astype(jnp.float32)  33.3 us
    all_gather x1, blocking collectives, per_device(): lax.all_gather(shares[2].astype(jnp.bfloat16), 'dp', axis=1, tiled=True)  31.8 us
  transfers between devices with their start and end apart: 12, of which 11 were waited for; matrix products, arithmetic and copies ran while one was open for 8% of the time, Pallas kernels for 0%

profile of v1, /device:TPU:0, one launch (start us, length us, event | category | flops | bytes accessed | tf_op | source)
XLA Modules:
  0.0 714.1 jit_solution(2763413078634612982)
XLA Ops:
  25.3 33.3 %all-reduce.7.cloned.1.call-done = bf16[394,768]{1,0:T(8,128)(2,1)} async-done(((bf16[394,768]{1,0:T(8,128)(2,1)}), bf16[394,768]{1,0:T(8,128)(2,1)}) %all-reduce.7.cloned.1.call-update) | async-done | bytes 605200 | tf_op jit(solution)/shard_map/psum | solution.py:96
  69.7 31.0 %all-reduce.9.cloned.1.call-done = bf16[394,768]{1,0:T(8,128)(2,1)} async-done(((bf16[394,768]{1,0:T(8,128)(2,1)}), bf16[394,768]{1,0:T(8,128)(2,1)}) %all-reduce.9.cloned.1.call-update) | async-done | bytes 605200 | tf_op jit(solution)/shard_map/psum | solution.py:117
  107.8 4.5 fusion.69
  112.2 3.8 fusion.34
  133.1 3.6 convolution_multiply_fusion
  141.3 26.9 %all-reduce.11.cloned.1.call-done = (bf16[394,768]{1,0:T(8,128)(2,1)}, bf16[394,768]{1,0:T(8,128)(2,1)}) async-done(((bf16[394,768]{1,0:T(8,128)(2,1)}, bf16[394,768]{1,0:T(8,128)(2,1)}), (bf16[394,768]{1,0:T(8,128)(2,1)}, bf16[394,768]{1,0:T(8,128)(2,1)})) %all-reduce.11.cloned.1.call-update) | async-done | bytes 1210384 | tf_op jit(solution)/shard_map/psum | solution.py:106
  177.1 3.1 convolution_multiply_fusion.2
  182.7 50.7 %reduce-scatter.29.cloned.1.call-done = f32[96,1]{1,0:T(8,128)} async-done(((f32[768,1]{1,0:T(8,128)}), f32[96,1]{1,0:T(8,128)}) %reduce-scatter.29.cloned.1.call-update) | async-done | bytes 400
  234.5 19.6 %all-reduce = bf16[768]{0:T(1024)(128)(2,1)S(1)} all-reduce(bf16[768]{0:T(1024)(128)(2,1)S(1)} %dynamic-update-slice), channel_id=1, replica_groups=mesh['dp'=8,'tensor'=4] {'dp'}, use_global_device_ids=true, to_apply=%add | all-reduce | flops 768 | bytes 3072
  254.9 17.1 %all-reduce.1 = bf16[2,192]{1,0:T(2,128)(2,1)S(1)} all-reduce(f32[2,192]{1,0:T(2,128)S(1)} %maximum_multiply_fusion.2), channel_id=4, replica_groups=mesh['dp'=8,'tensor'=4] {'dp'}, use_global_device_ids=true, to_apply=%region_22.0.clone | all-reduce | flops 384 | bytes 2304
  272.1 18.3 %all-gather.1 = bf16[8,24,2]{1,2,0:T(2,128)(2,1)S(1)} all-gather(bf16[1,24,2]{1,2,0:T(2,128)(2,1)S(1)} %fusion.60), channel_id=1, replica_groups=mesh['dp'=8,'tensor'=4] {'dp'}, dimensions={0}, use_global_device_ids=true | all-gather | bytes 864 | tf_op jit(solution)/shard_map/all_gather | solution.py:178
  291.1 7.3 %reduce-scatter.27.cloned.1.call-done = f32[96,3]{1,0:T(8,128)} async-done(((f32[768,3]{1,0:T(8,128)}), f32[96,3]{1,0:T(8,128)}) %reduce-scatter.27.cloned.1.call-update) | async-done | bytes 1168
  299.3 18.8 %all-gather.2 = bf16[8,96,3]{1,2,0:T(4,128)(2,1)S(1)} all-gather(bf16[1,96,3]{1,2,0:T(4,128)(2,1)S(1)} %bitcast.111), channel_id=1, replica_groups=mesh['dp'=8,'tensor'=4] {'dp'}, dimensions={0}, use_global_device_ids=true | all-gather | bytes 5184 | tf_op jit(solution)/shard_map/all_gather | solution.py:199
  318.1 52.9 %reduce-scatter.21.cloned.1.call-done = f32[768,96]{0,1:T(8,128)} async-done(((f32[768,768]{0,1:T(8,128)}), f32[768,96]{0,1:T(8,128)}) %reduce-scatter.21.cloned.1.call-update) | async-done | bytes 294928 | tf_op jit(solution)/shard_map/reduce_scatter | solution.py:171
  373.1 4.4 all-to-all-start
  377.7 82.0 %reduce-scatter.19.cloned.1.call-done = f32[768,96]{0,1:T(8,128)} async-done(((f32[768,768]{0,1:T(8,128)}), f32[768,96]{0,1:T(8,128)}) %reduce-scatter.19.cloned.1.call-update) | async-done | bytes 294928 | tf_op jit(solution)/shard_map/reduce_scatter | solution.py:169
  472.7 51.7 %reduce-scatter.23.cloned.1.call-done = f32[96,3]{1,0:T(8,128)} async-done(((f32[768,3]{1,0:T(8,128)}), f32[96,3]{1,0:T(8,128)}) %reduce-scatter.23.cloned.1.call-update) | async-done | bytes 1168
  525.2 18.7 %all-gather = bf16[8,96,3]{1,2,0:T(4,128)(2,1)S(1)} all-gather(bf16[1,96,3]{1,2,0:T(4,128)(2,1)S(1)} %bitcast.112), channel_id=1, replica_groups=mesh['dp'=8,'tensor'=4] {'dp'}, dimensions={0}, use_global_device_ids=true | all-gather | bytes 5184 | tf_op jit(solution)/shard_map/all_gather | solution.py:184
  544.6 45.4 %reduce-scatter.25.cloned.1.call-done = f32[96,192]{1,0:T(8,128)} async-done(((f32[768,192]{1,0:T(8,128)}), f32[96,192]{1,0:T(8,128)}) %reduce-scatter.25.cloned.1.call-update) | async-done | bytes 73744
  591.0 31.8 %all_gather.24 = bf16[192,768]{0,1:T(8,128)(2,1)S(1)} all-gather(bf16[192,96]{0,1:T(8,128)(2,1)S(1)} %copy.157), channel_id=1, replica_groups=mesh['dp'=8,'tensor'=4] {'dp'}, dimensions={1}, use_global_device_ids=true | all-gather | bytes 331776 | tf_op jit(solution)/shard_map/all_gather | solution.py:181
  623.8 36.1 %reduce-scatter.17.cloned.1.call-done = f32[768,72]{0,1:T(8,128)} async-done(((f32[768,576]{0,1:T(8,128)}), f32[768,72]{0,1:T(8,128)}) %reduce-scatter.17.cloned.1.call-update) | async-done | bytes 221200 | tf_op jit(solution)/shard_map/reduce_scatter | solution.py:165
  660.9 33.5 %all_gather.22 = bf16[768,576]{0,1:T(8,128)(2,1)S(1)} all-gather(bf16[768,72]{0,1:T(8,128)(2,1)S(1)} %convert_element_type.191), channel_id=1, replica_groups=mesh['dp'=8,'tensor'=4] {'dp'}, dimensions={1}, use_global_device_ids=true | all-gather | bytes 995328 | tf_op jit(solution)/shard_map/all_gather | solution.py:175
  698.6 3.0 copy.163
  701.6 3.2 all-gather.5.cloned.1.call-done
  (215 shorter events, 97.1 us)
Async XLA Ops:
  7.2 53.4 %copy-start = (bf16[768,768]{1,0:T(8,128)(2,1)S(1)}, bf16[768,768]{1,0:T(8,128)(2,1)}, u32[]{:S(2)}) copy-start(bf16[768,768]{1,0:T(8,128)(2,1)} %param.25) | copy-start | bytes 3538948
  7.2 3.0 copy-start.24
  7.2 3.0 copy-start.22
  7.2 51.3 %all-reduce.7.cloned.1.call-start = ((), (), s32[]{:S(2)}) async-start(), calls=%async_computation.8 | async-start | bytes 1228800 | tf_op jit(solution)/shard_map/psum | solution.py:96
  11.6 2.6 copy-start.8
  21.9 78.8 %all-reduce.9.cloned.1.call-start = ((), (), s32[]{:S(2)}) async-start(), calls=%async_computation.9 | async-start | bytes 1228800 | tf_op jit(solution)/shard_map/psum | solution.py:117
  23.3 35.3 %copy-start.25 = (f32[768]{0:T(1024)S(1)}, f32[768]{0:T(1024)}, u32[]{:S(2)}) copy-start(f32[768]{0:T(1024)} %param.22) | copy-start | bytes 9220
  25.1 35.1 %copy-start.31 = (f32[2]{0:T(128)}, f32[2]{0:T(128)S(1)}, u32[]{:S(2)}) copy-start(f32[2]{0:T(128)S(1)} %compare_convert_fusion) | copy-start | bytes 28
  66.5 101.6 %all-reduce.11.cloned.1.call-start = ((), (), s32[]{:S(2)}) async-start(), calls=%async_computation.18 | async-start | bytes 2457600 | tf_op jit(solution)/shard_map/psum | solution.py:106
  107.8 4.5 copy-start.19
  129.5 103.9 %reduce-scatter.29.cloned.1.call-start = ((), (), s32[]{:S(2)}) async-start(), calls=%async_computation.17 | async-start | bytes 442368
  132.0 166.4 %reduce-scatter.27.cloned.1.call-start = ((), (), s32[]{:S(2)}) async-start(), calls=%async_computation.16 | async-start | bytes 442368
  133.0 238.0 %reduce-scatter.21.cloned.1.call-start = ((), (), s32[]{:S(2)}) async-start(), calls=%async_computation.13 | async-start | bytes 2654208 | tf_op jit(solution)/shard_map/reduce_scatter | solution.py:171
  136.7 323.0 %reduce-scatter.19.cloned.1.call-start = ((), (), s32[]{:S(2)}) async-start(), calls=%async_computation.11 | async-start | bytes 2654208 | tf_op jit(solution)/shard_map/reduce_scatter | solution.py:169
  140.2 384.2 %reduce-scatter.23.cloned.1.call-start = ((), (), s32[]{:S(2)}) async-start(), calls=%async_computation.14 | async-start | bytes 442368
  168.1 3.2 copy-start.14
  171.3 418.6 %reduce-scatter.25.cloned.1.call-start = ((), (), s32[]{:S(2)}) async-start(), calls=%async_computation.15 | async-start | bytes 884736
  176.1 483.8 %reduce-scatter.17.cloned.1.call-start = ((), (), s32[]{:S(2)}) async-start(), calls=%async_computation.10 | async-start | bytes 1990656 | tf_op jit(solution)/shard_map/reduce_scatter | solution.py:165
  180.2 74.6 %copy-start.29 = (f32[3,64]{1,0:T(4,128)S(1)}, f32[3,64]{1,0:T(4,128)}, u32[]{:S(2)}) copy-start(f32[3,64]{1,0:T(4,128)} %get-tuple-element.107) | copy-start | bytes 2308
  373.1 89.0 %copy-start.26 = (f32[768]{0:T(1024)S(1)}, f32[768]{0:T(1024)}, u32[]{:S(2)}) copy-start(f32[768]{0:T(1024)} %param.28) | copy-start | bytes 9220
  373.1 322.6 %all-to-all-start = ((bf16[8,768,96]{1,2,0:T(8,128)(2,1)}), bf16[8,768,96]{1,2,0:T(8,128)(2,1)}, u32[]{:S(2)}, u32[]{:S(2)}) async-start(bf16[8,768,96]{1,2,0:T(8,128)(2,1)} %stack.64), calls=%async_computation.3 | async-start | bytes 2359296 | tf_op jit(solution)/shard_map/all_to_all | solution.py:194
  377.5 327.4 %all-gather.5.cloned.1.call-start = ((), (), s32[]{:S(2)}) async-start(), calls=%async_computation.12 | async-start | bytes 1327104 | tf_op jit(solution)/shard_map/all_gather | solution.py:187
  462.1 6.8 copy-start.10
  464.3 4.6 copy-start.2
  (27 other events, 37.5 us)
Sparse Core Ops, SparseCore 0:
  22.0 36.4 all-reduce.6
  66.6 34.0 all-reduce.8
  129.6 38.4 all-reduce.10
  171.2 62.1 reduce-scatter.28
  237.1 61.2 reduce-scatter.26
  302.3 68.6 reduce-scatter.20
  375.1 84.6 reduce-scatter.18
  463.0 61.2 reduce-scatter.22
  527.6 62.2 reduce-scatter.24
  593.8 66.0 reduce-scatter.16
  662.1 42.6 all-gather.4
